TPU v7x, 128 devices: a whole 4x4x4 slice. The times are simulated.
128 devices in a mesh: path: 4 (over z_lo, core), ctx: 32 (over x, z_hi, y).
Axes of the slice: x: 4, y: 4, z: 4 (z_hi: 2, z_lo: 2; z = z_hi * 2 + z_lo), core: 2. Of those that a mesh axis runs over, the one named last changes fastest.
Arguments:
- tokens: int32 [4096], P('ctx'), may hold values from 0 to 511
- sub_pos: int32 [512], P('ctx'), may hold values from 0 to 4095, as said below
- sub_base: int32 [512], P('ctx'), may hold values from 0 to 511
- embed: bfloat16 [512, 4096], replicated, may hold values from -6 to 6
- norm_gain: float32 [4096], replicated, may hold values from 0.1 to 1.9
- fir_taps: bfloat16 [3, 3, 4096], replicated, may hold values from -3.5 to 3.5
- long_filter: float32 [4096, 4096], P(None, 'ctx'), may hold values from -8 to 8
- skip_gain: float32 [4096], P('ctx'), may hold values from 0.5 to 1.5
- cotangent: bfloat16 [4096, 4096], P('ctx'), may hold values from -6 to 6
Outputs:
- path_grad: float32 [4096, 4096], P('ctx', 'path')
- attribution: float32 [4096, 4096], P('ctx', 'path')
Inputs may be any that keep to these rules, and one draw needn't show every extreme that they name: `sub_pos`: exactly one substituted position in each aligned block of 8 tokens, so the positions rise strictly.
All inputs are finite; a program needn't handle non-finite values.
Results may differ from a plain program's by a relative error of at most 0.0085.
Values may be sent and summed in bfloat16 or wider, within the bound.
A program may use at most 192 MiB of HBM per device.

v0:
```python
import jax
import jax.numpy as jnp
from jax import lax
from jax.sharding import PartitionSpec as P

PATH_DEV = 1
precise = lax.Precision.HIGH


def from_behind(block, axis, distance):
    devices = range(lax.axis_size(axis))
    route = [(i - distance, i) for i in devices if i - distance in devices]
    return lax.ppermute(block, axis, route)


def angle_tables(length):
    outer_size = 64
    inner_size = length // outer_size
    outer_idx = jnp.arange(outer_size, dtype=jnp.int32)
    inner_idx = jnp.arange(inner_size, dtype=jnp.int32)
    outer_angle = (
        2.0
        * jnp.pi
        / outer_size
        * (outer_idx[:, None] * outer_idx[None, :] % outer_size).astype(jnp.float32)
    )
    inner_angle = (
        2.0
        * jnp.pi
        / inner_size
        * (inner_idx[:, None] * inner_idx[None, :] % inner_size).astype(jnp.float32)
    )
    twist_angle = (
        2.0
        * jnp.pi
        / length
        * (outer_idx[:, None] * inner_idx[None, :] % length).astype(jnp.float32)
    )
    return (outer_angle, inner_angle, twist_angle)


def complex_table(angle, sign):
    cosine = jnp.cos(angle)
    sine = sign * jnp.sin(angle)
    return jnp.stack([jnp.stack([cosine, sine]), jnp.stack([-sine, cosine])])


def twisted(values, angle, sign):
    cosine = jnp.cos(angle)[None, :, :, None]
    sine = sign * jnp.sin(angle)[None, :, :, None]
    real_part = values[:, 0]
    imag_part = values[:, 1]
    return jnp.stack(
        [real_part * cosine - imag_part * sine, real_part * sine + imag_part * cosine], 1
    )


def spectrum(signal):
    batch, half, width = signal.shape
    length = 2 * half
    outer_angle, inner_angle, twist_angle = angle_tables(length)
    outer_size = outer_angle.shape[0]
    inner_size = inner_angle.shape[0]
    folded = signal.reshape(batch, outer_size // 2, inner_size, width)
    used = outer_angle[:, : outer_size // 2]
    outer_table = jnp.stack([jnp.cos(used), -jnp.sin(used)])
    first = jnp.einsum("rka,pabc->prkbc", outer_table, folded, precision=precise)
    turned = twisted(first, twist_angle, -1.0)
    return jnp.einsum(
        "prkbc,rsbm->pskmc", turned, complex_table(inner_angle, -1.0), precision=precise
    )


def inverse(spec):
    batch, parts, outer_size, inner_size, width = spec.shape
    length = outer_size * inner_size
    outer_angle, inner_angle, twist_angle = angle_tables(length)
    back = jnp.einsum("pskmc,stmb->ptkbc", spec, complex_table(inner_angle, 1.0), precision=precise)
    turned = twisted(back, twist_angle, 1.0)
    used = outer_angle[: outer_size // 2]
    outer_table = jnp.stack([jnp.cos(used), -jnp.sin(used)])
    result = jnp.einsum("rak,prkbc->pabc", outer_table, turned, precision=precise)
    return (result / length).reshape(batch, length // 2, width)


def long_conv(channels, filter_spec, skip_gain, adjoint):
    signal = channels.astype(jnp.float32)
    spec = spectrum(signal)
    sig_real = spec[:, 0]
    sig_imag = spec[:, 1]
    filt_real = filter_spec[:, 0]
    filt_imag = filter_spec[:, 1]
    if adjoint:
        prod_real = sig_real * filt_real + sig_imag * filt_imag
        prod_imag = sig_imag * filt_real - sig_real * filt_imag
    else:
        prod_real = sig_real * filt_real - sig_imag * filt_imag
        prod_imag = sig_real * filt_imag + sig_imag * filt_real
    return (inverse(jnp.stack([prod_real, prod_imag], 1)) + skip_gain * signal).astype(jnp.bfloat16)


def depthwise(signal, filters):
    return lax.conv_general_dilated(
        signal,
        filters[:, None, :],
        (1,),
        "VALID",
        dimension_numbers=("NWC", "WIO", "NWC"),
        feature_group_count=signal.shape[2],
        preferred_element_type=jnp.float32,
    )


def to_channels(values):
    return lax.all_to_all(values, "ctx", split_axis=2, concat_axis=1, tiled=True)


def to_tokens(values):
    return lax.all_to_all(values, "ctx", split_axis=1, concat_axis=2, tiled=True)


def body(tokens, sub_pos, sub_base, embed, norm_gain, fir_taps, long_filter, skip_gain, cotangent):
    tok_rows = tokens.shape[0]
    width = embed.shape[1]
    reach = fir_taps.shape[1] - 1
    path_size = lax.axis_size("path")
    points = PATH_DEV * path_size
    in_block = jnp.arange(8, dtype=jnp.int32)[None, :] == (sub_pos % 8)[:, None]
    base_ids = jnp.where(in_block, sub_base[:, None], tokens.reshape(-1, 8)).reshape(-1)
    emb_tok = jnp.take(embed, tokens, axis=0).astype(jnp.float32)
    emb_base = jnp.take(embed, base_ids, axis=0).astype(jnp.float32)
    difference = emb_tok - emb_base
    first_point = lax.axis_index("path") * PATH_DEV
    alphas = (
        (first_point + jnp.arange(PATH_DEV, dtype=jnp.int32)).astype(jnp.float32) + 0.5
    ) / points
    inputs = emb_base[None] + alphas[:, None, None] * difference[None]
    inv_rms = lax.rsqrt(jnp.mean(inputs * inputs, -1, keepdims=True) + 1e-06)
    normed = (inputs * inv_rms * norm_gain).astype(jnp.bfloat16)
    earlier = from_behind(normed[:, tok_rows - reach :], "ctx", 1)
    extended = jnp.concatenate([earlier, normed], 1)
    flipped = fir_taps[:, ::-1, :]
    q_feat = depthwise(extended, flipped[0])
    k_feat = depthwise(extended, flipped[1])
    v_feat = depthwise(extended, flipped[2])
    gated = (k_feat * v_feat).astype(jnp.bfloat16)
    upstream = cotangent.astype(jnp.float32)[None]
    grad_y = (upstream * q_feat).astype(jnp.bfloat16)
    filter_spec = spectrum(long_filter[None])
    conv_out = to_tokens(long_conv(to_channels(gated), filter_spec, skip_gain, False))
    grad_z = to_tokens(long_conv(to_channels(grad_y), filter_spec, skip_gain, True))
    grad_z32 = grad_z.astype(jnp.float32)
    grad_q = (upstream * conv_out.astype(jnp.float32)).astype(jnp.bfloat16)
    grad_k = (grad_z32 * v_feat).astype(jnp.bfloat16)
    grad_v = (grad_z32 * k_feat).astype(jnp.bfloat16)
    grads = (grad_q, grad_k, grad_v)
    heads = jnp.stack([grad_q[:, :reach], grad_k[:, :reach], grad_v[:, :reach]])
    later = from_behind(heads, "ctx", -1)
    grad_norm = sum(
        (
            depthwise(jnp.concatenate([grads[index], later[index]], 1), fir_taps[index])
            for index in range(3)
        )
    )
    scaled = norm_gain * grad_norm
    grad_in = inv_rms * scaled - inputs * inv_rms**3 * jnp.mean(inputs * scaled, -1, keepdims=True)
    summed = lax.psum_scatter(
        jnp.sum(grad_in, 0).astype(jnp.bfloat16), "path", scatter_dimension=1, tiled=True
    ).astype(jnp.float32)
    path_grad = summed / points
    share = width // path_size
    columns = lax.dynamic_slice_in_dim(difference, lax.axis_index("path") * share, share, 1)
    return (path_grad, columns * path_grad)


def solution(mesh):
    return jax.shard_map(
        body,
        mesh=mesh,
        in_specs=(
            P("ctx"),
            P("ctx"),
            P("ctx"),
            P(),
            P(),
            P(),
            P(None, "ctx"),
            P("ctx"),
            P("ctx", None),
        ),
        out_specs=(P("ctx", "path"), P("ctx", "path")),
        check_vma=False,
    )
```

profile of v0, /device:TPU:1, one launch (start us, length us, event | category | flops | bytes accessed | tf_op | source)
XLA Modules:
  0.0 581.1 jit_solution(8248613599338435576)
XLA Ops:
  10.4 4.9 gather_fusion
  15.3 6.3 %gather_fusion.1 = bf16[128,4096]{1,0:T(8,128)(2,1)} fusion(bf16[512,4096]{1,0:T(8,128)(2,1)} %param.14, s32[1024]{0:T(1024)S(1)} %pad_clamp_fusion), kind=kCustom, calls=%fused_computation.1.clone | custom fusion | bytes 2097664 | tf_op jit(solution)/shard_map/jit(_take)/gather | solution.py:130
  28.2 4.2 collective-permute-start
  35.8 9.5 %slice.109 = bf16[1,3,4096]{2,1,0:T(4,128)(2,1)} reverse(bf16[1,3,4096]{2,1,0:T(4,128)(2,1)S(1)} %get-tuple-element.38), dimensions={1} | reverse | bytes 49152 | tf_op jit(solution)/shard_map/slice | solution.py:145
  45.3 9.5 %slice.107 = bf16[1,3,4096]{2,1,0:T(4,128)(2,1)} reverse(bf16[1,3,4096]{2,1,0:T(4,128)(2,1)S(1)} %get-tuple-element.36), dimensions={1} | reverse | bytes 49152 | tf_op jit(solution)/shard_map/slice | solution.py:144
  54.8 9.5 %slice.124 = bf16[1,3,4096]{2,1,0:T(4,128)(2,1)} reverse(bf16[1,3,4096]{2,1,0:T(4,128)(2,1)S(1)} %get-tuple-element.37), dimensions={1} | reverse | bytes 49152 | tf_op jit(solution)/shard_map/slice | solution.py:143
  83.6 5.5 copy.169
  89.7 24.4 %reduce.3 = bf16[4096,128]{1,0:T(8,128)(2,1)} reduce(bf16[4096,1,128]{2,1,0:T(2,128)(2,1)} %bitcast.293, bf16[]{:T(256)} %broadcast.627), dimensions={1}, to_apply=%bitcast.262.reduce_sub_computation | reduce | bytes 2097154
  116.2 10.4 %all-to-all-start = ((bf16[32,2,8192]{2,1,0:T(2,128)(2,1)}), bf16[32,2,8192]{2,1,0:T(2,128)(2,1)}, u32[]{:S(2)}, u32[]{:S(2)}) async-start(bf16[32,2,8192]{2,1,0:T(2,128)(2,1)} %reshape.653), calls=%async_computation | async-start | bytes 2097152 | tf_op jit(solution)/shard_map/all_to_all | solution.py:115
  131.4 3.5 reshape.576
  135.0 3.1 slice.167
  142.8 17.0 %copy.315 = bf16[1,128,4096]{1,0,2:T(2,128)(2,1)} copy(bf16[1,128,4096]{1,2,0:T(8,128)(2,1)S(1)} %fusion.47) | data formatting | bytes 2097152 | tf_op jit(solution)/shard_map/convert_element_type | solution.py:148
  159.9 23.5 %reduce.4 = bf16[4096,128]{1,0:T(8,128)(2,1)S(1)} reduce(bf16[4096,1,128]{2,1,0:T(2,128)(2,1)} %bitcast.295, bf16[]{:T(256)} %broadcast.627), dimensions={1}, to_apply=%bitcast.282.reduce_sub_computation | reduce | bytes 2097154
  184.5 9.4 %all-to-all-start.2 = ((bf16[32,2,8192]{2,1,0:T(2,128)(2,1)}), bf16[32,2,8192]{2,1,0:T(2,128)(2,1)S(1)}, u32[]{:S(2)}, u32[]{:S(2)}) async-start(bf16[32,2,8192]{2,1,0:T(2,128)(2,1)} %reshape.649), calls=%async_computation.2 | async-start | bytes 2097152 | tf_op jit(solution)/shard_map/all_to_all | solution.py:115
  194.8 6.9 %convolution_bitcast_fusion.1 = f32[1,2,64,128,128]{4,2,1,3,0:T(8,128)} fusion(f32[32,128,128,1]{2,1,0,3:T(8,128)S(1)} %bitcast.284, f32[1,64,32]{1,2,0:T(8,128)S(1)} %get-tuple-element.49, f32[1,64,32]{1,2,0:T(8,128)S(1)} %get-tuple-element.48), kind=kOutput, calls=%fused_computation.61 | convolution fusion | flops 402657280 | bytes 10502144 | tf_op jit(solution)/shard_map/rka,pabc->prkbc/dot_general | solution.py:67
  201.8 4.3 reshape.654
  209.1 6.4 %convolution_bitcast_fusion.2 = f32[1,2,64,128,128]{4,2,1,3,0:T(8,128)} fusion(bf16[1,128,32,128]{3,2,1,0:T(8,128)(2,1)S(1)} %copy.238, f32[1,64,32]{1,2,0:T(8,128)} %copy-done.24, f32[1,64,32]{1,2,0:T(8,128)S(1)} %get-tuple-element.48), kind=kOutput, calls=%fused_computation.62 | convolution fusion | flops 402657280 | bytes 9453568 | tf_op jit(solution)/shard_map/rka,pabc->prkbc/dot_general | solution.py:67
  219.4 3.1 convolution_bitcast_fusion
  223.3 12.8 %multiply_subtract_fusion.6 = (f32[1,1,64,128,128]{4,2,1,3,0:T(8,128)}, f32[1,1,64,128,128]{4,2,1,3,0:T(8,128)}, f32[1,1,64,128,128]{4,2,1,3,0:T(8,128)}, f32[1,...) fusion(f32[1,2,64,128,128]{4,2,1,3,0:T(8,128)} %convolution_bitcast_fusion.2, ...), kind=kLoop, calls=%fused_computation.54 | loop fusion | flops 18874368 | bytes 50397184 | tf_op jit(solution)/shard_map/sub | solution.py:54
  236.1 4.1 maximum_bitcast_fusion.5
  240.2 12.2 %fusion.33 = f32[1,2,64,128,128]{4,3,2,1,0:T(8,128)S(1)} fusion(f32[2,64,128,128]{3,1,0,2:T(8,128)} %maximum_bitcast_fusion.5, f32[1,2,128,128]{2,3,0,1:T(8,128)S(1)} %get-tuple-element.40, f32[1,2,128,128]{2,3,0,1:T(8,128)S(1)} %get-tuple-element.41), kind=kOutput, calls=%fused_computation.58 | convolution fusion | flops 3221291008 | bytes 17039360 | tf_op jit(solution)/shard_map/prkbc,rsbm->pskmc/dot_general | solution.py:69
  252.4 10.1 %maximum_bitcast_fusion = (f32[2,64,128,128]{3,1,0,2:T(8,128)}, f32[2,64,128,128]{3,1,0,2:T(8,128)}) fusion(f32[1,1,64,128,128]{4,2,1,3,0:T(8,128)} %get-tuple-element.14, f32[1,1,64,128,128]{4,2,1,3,0:T(8,128)S(1)} %copy-done.9, f32[1,1,64,128,128]{4,2,1,3,0:T(8,128)} %get-tuple-element.29, f32[1,1,64,128,128]{4,2,1,3,0:T(8,128)} %get-tuple-element.30), kind=kLoop, calls=%fused_computation.2 | loop fusion | flops 4194304 | bytes 33554432 | tf_op jit(solution)/shard_map/reshape.21
  262.5 14.1 %fusion.27 = f32[1,2,64,128,128]{4,3,2,1,0:T(8,128)} fusion(f32[2,64,128,128]{3,1,0,2:T(8,128)} %get-tuple-element.58, f32[1,2,128,128]{2,3,0,1:T(8,128)S(1)} %get-tuple-element.40, f32[1,2,128,128]{2,3,0,1:T(8,128)S(1)} %get-tuple-element.41), kind=kOutput, calls=%fused_computation.56 | convolution fusion | flops 3221291008 | bytes 17039360 | tf_op jit(solution)/shard_map/prkbc,rsbm->pskmc/dot_general | solution.py:69
  276.6 13.9 %fusion.24 = f32[1,2,64,128,128]{4,3,2,1,0:T(8,128)} fusion(f32[2,64,128,128]{3,1,0,2:T(8,128)S(1)} %copy-done.2, f32[1,2,128,128]{2,3,0,1:T(8,128)S(1)} %get-tuple-element.40, f32[1,2,128,128]{2,3,0,1:T(8,128)S(1)} %get-tuple-element.41), kind=kOutput, calls=%fused_computation.55 | convolution fusion | flops 3221291008 | bytes 17039360 | tf_op jit(solution)/shard_map/prkbc,rsbm->pskmc/dot_general | solution.py:69
  290.5 11.8 %multiply_subtract_fusion.4 = (f32[1,1,64,128,128]{4,3,2,1,0:T(8,128)}, f32[1,1,64,128,128]{4,3,2,1,0:T(8,128)}, f32[1,1,64,128,128]{4,3,2,1,0:T(8,128)}, f32[1,1,64,128,128]{4,3,2,1,0:T(8,128)}) fusion(f32[1,2,64,128,128]{4,3,2,1,0:T(8,128)} %fusion.24, f32[1,2,64,128,128]{4,3,2,1,0:T(8,128)} %fusion.27, f32[1,2,64,128,128]{4,3,2,1,0:T(8,128)S(1)} %fusion.33), kind=kLoop, calls=%fused_computation.50 | loop fusion | flops 12582912 | bytes 41943040 | tf_op jit(solution)/shard_map/sub | solution.py:97
  302.4 7.0 %fusion.36 = f32[2,128,64,128]{3,1,2,0:T(8,128)S(1)} fusion(f32[1,1,64,128,128]{4,3,2,1,0:T(8,128)} %get-tuple-element.21, f32[1,1,64,128,128]{4,3,2,1,0:T(8,128)} %get-tuple-element.22, f32[1,2,128,128]{2,3,1,0:T(8,128)S(1)} %copy-done.31, f32[1,2,128,128]{2,3,1,0:T(8,128)S(1)} %copy-done.30), kind=kOutput, calls=%fused_computation.59 | convolution fusion | flops 3223388160 | bytes 17039360 | tf_op jit(solution)/shard_map/pskmc,stmb->ptkbc/dot_general | solution.py:78
  309.3 4.9 copy.312
  314.2 8.9 %fusion.30 = f32[2,128,64,128]{3,1,2,0:T(8,128)} fusion(f32[1,1,64,128,128]{4,3,2,1,0:T(8,128)} %get-tuple-element.8, f32[1,1,64,128,128]{4,3,2,1,0:T(8,128)} %get-tuple-element.7, f32[1,2,128,128]{2,3,1,0:T(8,128)S(1)} %copy-done.31, f32[1,2,128,128]{2,3,1,0:T(8,128)S(1)} %copy-done.30), kind=kOutput, calls=%fused_computation.57 | convolution fusion | flops 3223388160 | bytes 17039360 | tf_op jit(solution)/shard_map/pskmc,stmb->ptkbc/dot_general | solution.py:78
  323.1 8.3 %copy.313 = f32[2,128,64,128]{3,2,0,1:T(8,128)S(1)} copy(f32[2,128,64,128]{3,1,2,0:T(8,128)} %fusion.30) | data formatting | bytes 16777216 | tf_op jit(solution)/shard_map/pskmc,stmb->ptkbc/dot_general | solution.py:78
  331.4 6.8 %multiply_subtract_fusion.3 = (f32[1,1,64,128,128]{4,2,1,3,0:T(8,128)S(1)}, f32[1,1,64,128,128]{4,2,1,3,0:T(8,128)}, f32[1,1,64,128,128]{4,2,1,3,0:T(8,128)}, f32[1,1,64,128,128]{4,2,1,3,0:T(8,128)}) fusion(f32[1,2,64,128,128]{4,2,1,3,0:T(8,128)S(1)} %bitcast.286, f32[64,128]{0,1:T(8,128)S(1)} %copy-done.26, f32[64,128]{0,1:T(8,128)S(1)} %fusion.115, ...), kind=kLoop, calls=%fused_computation.48 | loop fusion | flops 12582912 | bytes 33619968 | tf_op jit(solution)/shard_map/sub | solution.py:54
  338.2 4.8 fusion.54
  353.2 16.7 %copy.314 = bf16[1,4096,128]{2,0,1:T(2,128)(2,1)S(1)} copy(bf16[1,4096,128]{2,1,0:T(8,128)(2,1)S(1)} %get-tuple-element.53) | data formatting | bytes 2097152 | tf_op jit(solution)/shard_map/convert_element_type | solution.py:99
  369.8 22.7 %reduce.5 = bf16[4096,128]{1,0:T(8,128)(2,1)S(1)} reduce(bf16[4096,1,128]{2,1,0:T(2,128)(2,1)S(1)} %bitcast.296, bf16[]{:T(256)} %broadcast.627), dimensions={1}, to_apply=%bitcast.281.reduce_sub_computation | reduce | bytes 2097154
  393.6 9.5 %all-to-all-start.3 = ((bf16[32,2,8192]{2,1,0:T(2,128)(2,1)}), bf16[32,2,8192]{2,1,0:T(2,128)(2,1)S(1)}, u32[]{:S(2)}, u32[]{:S(2)}) async-start(bf16[32,2,8192]{2,1,0:T(2,128)(2,1)} %reshape.651), calls=%async_computation.3 | async-start | bytes 2097152 | tf_op jit(solution)/shard_map/all_to_all | solution.py:119
  403.1 4.8 copy.198
  407.9 3.0 copy.200
  410.9 3.6 reshape.580
  417.9 3.5 reshape.578
  424.9 3.2 copy.316
  428.1 23.4 %reduce.6 = bf16[4096,128]{1,0:T(8,128)(2,1)} reduce(bf16[4096,1,128]{2,1,0:T(2,128)(2,1)S(1)} %bitcast.294, bf16[]{:T(256)} %broadcast.627), dimensions={1}, to_apply=%bitcast.283.reduce_sub_computation | reduce | bytes 2097154
  453.6 9.5 %all-to-all-start.1 = ((bf16[32,2,8192]{2,1,0:T(2,128)(2,1)}), bf16[32,2,8192]{2,1,0:T(2,128)(2,1)}, u32[]{:S(2)}, u32[]{:S(2)}) async-start(bf16[32,2,8192]{2,1,0:T(2,128)(2,1)} %reshape.655), calls=%async_computation.1 | async-start | bytes 2097152 | tf_op jit(solution)/shard_map/all_to_all | solution.py:119
  466.9 3.2 fusion.50
  471.5 5.9 %all-to-all-done.1 = bf16[32,2,8192]{2,1,0:T(2,128)(2,1)} async-done(((bf16[32,2,8192]{2,1,0:T(2,128)(2,1)}), bf16[32,2,8192]{2,1,0:T(2,128)(2,1)}, u32[]{:S(2)}, u32[]{:S(2)}) %all-to-all-start.1) | async-done | bytes 1048608 | tf_op jit(solution)/shard_map/all_to_all | solution.py:119
  477.4 4.3 reshape.656
  492.3 3.5 collective-permute-done.1
  500.3 3.8 copy.256
  536.5 3.7 reshape.574
  545.1 26.8 %reduce-scatter.2.cloned.1.call-done = bf16[128,1024]{1,0:T(8,128)(2,1)} async-done(((bf16[128,4096]{1,0:T(8,128)(2,1)}), bf16[128,1024]{1,0:T(8,128)(2,1)}) %reduce-scatter.2.cloned.1.call-update) | async-done | bytes 262160 | tf_op jit(solution)/shard_map/reduce_scatter | solution.py:167
  (215 shorter events, 133.9 us)
Async XLA Ops:
  7.2 187.6 %copy-start = (f32[4096,128]{1,0:T(8,128)S(1)}, f32[4096,128]{1,0:T(8,128)}, u32[]{:S(2)}) copy-start(f32[4096,128]{1,0:T(8,128)} %param.17) | copy-start | bytes 6291460
  10.3 13.9 %copy-start.41 = (pred[128]{0:T(512)(128)(4,1)}, pred[128]{0:T(512)(128)(4,1)S(1)}, u32[]{:S(2)}) copy-start(pred[128]{0:T(512)(128)(4,1)S(1)} %get-tuple-element.5) | copy-start | bytes 388
  10.3 13.9 %copy-start.43 = (pred[128]{0:T(512)(128)(4,1)}, pred[128]{0:T(512)(128)(4,1)S(1)}, u32[]{:S(2)}) copy-start(pred[128]{0:T(512)(128)(4,1)S(1)} %get-tuple-element.54) | copy-start | bytes 388
  15.3 9.0 %copy-start.3 = (bf16[128,4096]{1,0:T(8,128)(2,1)}, bf16[128,4096]{1,0:T(8,128)(2,1)S(1)}, u32[]{:S(2)}) copy-start(bf16[128,4096]{1,0:T(8,128)(2,1)S(1)} %gather_fusion) | copy-start | bytes 3145732
  15.3 9.0 %copy-start.39 = (f32[4096]{0:T(1024)S(1)}, f32[4096]{0:T(1024)}, u32[]{:S(2)}) copy-start(f32[4096]{0:T(1024)} %param.15) | copy-start | bytes 49156
  21.6 2.6 copy-start.5
  24.3 2.2 copy-start.45
  24.3 9.2 %copy-start.32 = (bf16[3,3,4096]{2,1,0:T(4,128)(2,1)S(1)}, bf16[3,3,4096]{2,1,0:T(4,128)(2,1)}, u32[]{:S(2)}) copy-start(bf16[3,3,4096]{2,1,0:T(4,128)(2,1)} %param.16) | copy-start | bytes 221188
  28.2 37.8 %collective-permute-start = (bf16[1,2,4096]{2,1,0:T(2,128)(2,1)}, bf16[1,2,4096]{2,1,0:T(2,128)(2,1)S(1)}, u32[]{:S(2)}, u32[]{:S(2)}) collective-permute-start(bf16[1,2,4096]{2,1,0:T(2,128)(2,1)} %slice.151), channel_id=1, source_target_pairs={{0,1},{1,2},{2,3},{3,4},{4,5},{5,6},{6,7},{7,8},{8,9},{9,10},{10,1... | collective-permute-start | bytes 49160 | tf_op jit(solution)/shard_map/ppermute | solution.py:13
  32.4 36.5 %copy-start.27 = (f32[64,64]{0,1:T(8,128)}, f32[64,64]{0,1:T(8,128)S(1)}, u32[]{:S(2)}) copy-start(f32[64,64]{0,1:T(8,128)S(1)} %fusion.113) | copy-start | bytes 49156
  34.2 160.5 %copy-start.24 = (f32[1,64,32]{1,2,0:T(8,128)}, f32[1,64,32]{1,2,0:T(8,128)S(1)}, u32[]{:S(2)}) copy-start(f32[1,64,32]{1,2,0:T(8,128)S(1)} %get-tuple-element.49) | copy-start | bytes 24580
  65.9 75.1 %copy-start.11 = (bf16[128,4096]{0,1:T(8,128)(2,1)}, bf16[128,4096]{0,1:T(8,128)(2,1)S(1)}, u32[]{:S(2)}) copy-start(bf16[128,4096]{0,1:T(8,128)(2,1)S(1)} %copy.162) | copy-start | bytes 3145732
  68.8 5.0 copy-start.49
  71.7 2.1 copy-start.38
  74.5 2.2 copy-start.17
  114.1 12.6 %copy-start.36 = (bf16[1,3,4096]{2,1,0:T(4,128)(2,1)S(1)}, bf16[1,3,4096]{2,1,0:T(4,128)(2,1)}, u32[]{:S(2)}) copy-start(bf16[1,3,4096]{2,1,0:T(4,128)(2,1)} %slice.124) | copy-start | bytes 73732
  116.2 68.3 %all-to-all-start = ((bf16[32,2,8192]{2,1,0:T(2,128)(2,1)}), bf16[32,2,8192]{2,1,0:T(2,128)(2,1)}, u32[]{:S(2)}, u32[]{:S(2)}) async-start(bf16[32,2,8192]{2,1,0:T(2,128)(2,1)} %reshape.653), calls=%async_computation | async-start | bytes 2097152 | tf_op jit(solution)/shard_map/all_to_all | solution.py:115
  184.5 32.7 %all-to-all-start.2 = ((bf16[32,2,8192]{2,1,0:T(2,128)(2,1)}), bf16[32,2,8192]{2,1,0:T(2,128)(2,1)S(1)}, u32[]{:S(2)}, u32[]{:S(2)}) async-start(bf16[32,2,8192]{2,1,0:T(2,128)(2,1)} %reshape.649), calls=%async_computation.2 | async-start | bytes 2097152 | tf_op jit(solution)/shard_map/all_to_all | solution.py:115
  194.8 6.9 %copy-start.28 = (f32[64,64]{0,1:T(8,128)S(1)}, f32[64,64]{0,1:T(8,128)}, u32[]{:S(2)}) copy-start(f32[64,64]{0,1:T(8,128)} %copy-done.27) | copy-start | bytes 49156
  240.2 12.2 %copy-start.9 = (f32[1,1,64,128,128]{4,2,1,3,0:T(8,128)S(1)}, f32[1,1,64,128,128]{4,2,1,3,0:T(8,128)}, u32[]{:S(2)}) copy-start(f32[1,1,64,128,128]{4,2,1,3,0:T(8,128)} %get-tuple-element.13) | copy-start | bytes 12582916
  262.5 14.1 %copy-start.2 = (f32[2,64,128,128]{3,1,0,2:T(8,128)S(1)}, f32[2,64,128,128]{3,1,0,2:T(8,128)}, u32[]{:S(2)}) copy-start(f32[2,64,128,128]{3,1,0,2:T(8,128)} %get-tuple-element.57) | copy-start | bytes 25165828
  290.5 11.8 %copy-start.30 = (f32[1,2,128,128]{2,3,1,0:T(8,128)S(1)}, f32[1,2,128,128]{2,3,1,0:T(8,128)}, u32[]{:S(2)}) copy-start(f32[1,2,128,128]{2,3,1,0:T(8,128)} %get-tuple-element.39) | copy-start | bytes 393220
  290.5 11.8 %copy-start.31 = (f32[1,2,128,128]{2,3,1,0:T(8,128)S(1)}, f32[1,2,128,128]{2,3,1,0:T(8,128)}, u32[]{:S(2)}) copy-start(f32[1,2,128,128]{2,3,1,0:T(8,128)} %get-tuple-element.42) | copy-start | bytes 393220
  323.1 8.3 %copy-start.26 = (f32[64,128]{0,1:T(8,128)S(1)}, f32[64,128]{0,1:T(8,128)}, u32[]{:S(2)}) copy-start(f32[64,128]{0,1:T(8,128)} %fusion.114) | copy-start | bytes 98308
  343.0 2.2 copy-start.10
  347.6 1.6 copy-start.15
  393.6 60.1 %all-to-all-start.3 = ((bf16[32,2,8192]{2,1,0:T(2,128)(2,1)}), bf16[32,2,8192]{2,1,0:T(2,128)(2,1)S(1)}, u32[]{:S(2)}, u32[]{:S(2)}) async-start(bf16[32,2,8192]{2,1,0:T(2,128)(2,1)} %reshape.651), calls=%async_computation.3 | async-start | bytes 2097152 | tf_op jit(solution)/shard_map/all_to_all | solution.py:119
  403.1 4.8 copy-start.18
  414.5 1.6 slice-start
  421.5 1.6 slice-start.1
  453.6 23.8 %all-to-all-start.1 = ((bf16[32,2,8192]{2,1,0:T(2,128)(2,1)}), bf16[32,2,8192]{2,1,0:T(2,128)(2,1)}, u32[]{:S(2)}, u32[]{:S(2)}) async-start(bf16[32,2,8192]{2,1,0:T(2,128)(2,1)} %reshape.655), calls=%async_computation.1 | async-start | bytes 2097152 | tf_op jit(solution)/shard_map/all_to_all | solution.py:119
  463.1 108.7 %reduce-scatter.2.cloned.1.call-start = ((), (), s32[]{:S(2)}) async-start(), calls=%async_computation.5 | async-start | bytes 1310720 | tf_op jit(solution)/shard_map/reduce_scatter | solution.py:167
  483.5 3.0 copy-start.12
  488.3 9.0 %copy-start.14 = (bf16[1,128,4096]{1,2,0:T(8,128)(2,1)S(1)}, bf16[1,128,4096]{1,2,0:T(8,128)(2,1)}, u32[]{:S(2)}) copy-start(bf16[1,128,4096]{1,2,0:T(8,128)(2,1)} %copy-done.13) | copy-start | bytes 3145732
  491.0 4.8 collective-permute-start.1
  527.8 2.4 copy-start.35
  527.8 2.4 copy-start.50
  530.2 1.2 copy-start.23
  531.5 1.2 copy-start.40
  536.5 3.7 copy-start.4
  536.5 3.7 copy-start.6
  536.5 3.7 copy-start.42
  536.5 3.7 copy-start.44
  540.2 2.5 copy-start.7
  540.2 2.6 copy-start.8
  540.2 2.6 copy-start.46
  540.3 2.6 copy-start.47
  542.8 31.2 %copy-start.1 = (f32[4096,128]{1,0:T(8,128)S(1)}, f32[4096,128]{1,0:T(8,128)}, u32[]{:S(2)}) copy-start(f32[4096,128]{1,0:T(8,128)} %param.17) | copy-start | bytes 6291460
  (12 other events, 12.7 us)
Sparse Core Ops, SparseCore 0:
  545.2 26.6 reduce-scatter.1
where the time goes:
time: 589 us; the launch traced here: 581 us
  local copies, waits for them, and re-layouts  221 us (38%)
  other arithmetic  179 us (30%)
  matrix products  86 us (15%)
  starting transfers between devices  44.2 us (8%)
  waiting for transfers between devices  36.3 us (6%)
  between operations  15.1 us (3%)
    unnamed x4, other arithmetic  94 us
    unnamed x123, local copies, waits for them, and re-layouts  46.4 us
    conv_general_dilated x23, local copies, waits for them, and re-layouts, depthwise(): lax.conv_general_dilated(signal, filters[:, None, :], (1,), 'VALID', dime...  42.3 us
    dot_general x3, matrix products, spectrum(): jnp.einsum('prkbc,rsbm->pskmc', turned, complex_table(inner_angle, -1.0),...  40.2 us
    reduce_scatter x1, waiting for transfers between devices, body(): lax.psum_scatter(jnp.sum(grad_in, 0).astype(jnp.bfloat16), 'path', scatte...  26.8 us
    convert_element_type x2, local copies, waits for them, and re-layouts, long_conv(): (inverse(jnp.stack([prod_real, prod_imag], 1)) + skip_gain * signal).asty...  19.8 us
    all_to_all x2, starting transfers between devices, to_channels(): lax.all_to_all(values, 'ctx', split_axis=2, concat_axis=1, tiled=True)  19.8 us
    sub x2, other arithmetic, twisted(): real_part * cosine - imag_part * sine  19.6 us
  transfers between devices with their start and end apart: 7, of which 3 were waited for; matrix products, arithmetic and copies ran while one was open for 29% of the time, Pallas kernels for 0%

commit v1 on v0

--- a/solution.py
+++ b/solution.py
@@ -5,6 +5,16 @@
 
 PATH_DEV = 1
 precise = lax.Precision.HIGH
+
+
+def sections_track(content, group_axis):
+    val = jnp.concatenate(
+        lax.all_to_all(
+            jnp.stack(jnp.split(content, lax.axis_size(group_axis), 2), 0), group_axis, 0, 0
+        ),
+        1,
+    )
+    return val
 
 
 def from_behind(block, axis, distance):
@@ -112,7 +122,7 @@
 
 
 def to_channels(values):
-    return lax.all_to_all(values, "ctx", split_axis=2, concat_axis=1, tiled=True)
+    return sections_track(values, "ctx")
 
 
 def to_tokens(values):

time: 589 us -> 544 us (0.924)
  other arithmetic: 179 us -> 128 us
    unnamed x4 -> x2, other arithmetic: 94 us -> 44.8 us
    convert_element_type x4 -> x66, local copies, waits for them, and re-layouts: 12.4 us -> 40.9 us  [body(): gated = (k_feat * v_feat).astype(jnp.bfloat16)]
    unnamed x123 -> x167, local copies, waits for them, and re-layouts: 46.4 us -> 72.1 us
    convert_element_type x4 -> x0, local copies, waits for them, and re-layouts: 21.3 us -> none  [the longest x1 17 us: body(): grad_y = (upstream * q_feat).astype(jnp.bfloat16)]
    conv_general_dilated x23 -> x14, local copies, waits for them, and re-layouts: 42.3 us -> 25.7 us  [depthwise(): lax.conv_general_dilated(signal, filters[:, None, :], (1,), 'VALID', dime...]
    convert_element_type x2, local copies, waits for them, and re-layouts: 19.8 us -> 33.3 us  [long_conv(): (inverse(jnp.stack([prod_real, prod_imag], 1)) + skip_gain * signal).asty...]
    slice x1, local copies, waits for them, and re-layouts: 9.48 us -> 0.81 us  [body(): v_feat = depthwise(extended, flipped[2])]
    slice x1, local copies, waits for them, and re-layouts: 9.48 us -> 0.84 us  [body(): k_feat = depthwise(extended, flipped[1])]
  transfers between devices with their start and end apart: 7 -> 7, of which waited for: 3 -> 3; matrix products, arithmetic and copies ran while one was open for 29% -> 33% of each run, Pallas kernels for 0% -> 0%
where the time goes in v1:
time: 544 us; the launch traced here: 533 us
  local copies, waits for them, and re-layouts  223 us (41%)
  other arithmetic  128 us (24%)
  matrix products  86.5 us (16%)
  starting transfers between devices  44.7 us (8%)
  waiting for transfers between devices  35.5 us (7%)
  between operations  15.5 us (3%)
    unnamed x167, local copies, waits for them, and re-layouts  72.1 us
    unnamed x2, other arithmetic  44.8 us
    convert_element_type x66, local copies, waits for them, and re-layouts, body(): gated = (k_feat * v_feat).astype(jnp.bfloat16)  40.9 us
    dot_general x3, matrix products, spectrum(): jnp.einsum('prkbc,rsbm->pskmc', turned, complex_table(inner_angle, -1.0),...  40 us
    convert_element_type x2, local copies, waits for them, and re-layouts, long_conv(): (inverse(jnp.stack([prod_real, prod_imag], 1)) + skip_gain * signal).asty...  33.3 us
    reduce_scatter x1, waiting for transfers between devices, body(): lax.psum_scatter(jnp.sum(grad_in, 0).astype(jnp.bfloat16), 'path', scatte...  26.7 us
    conv_general_dilated x14, local copies, waits for them, and re-layouts, depthwise(): lax.conv_general_dilated(signal, filters[:, None, :], (1,), 'VALID', dime...  25.7 us
    all_to_all x2, starting transfers between devices, sections_track(): lax.all_to_all(jnp.stack(jnp.split(content, lax.axis_size(group_axis), 2)...  19.8 us
  transfers between devices with their start and end apart: 7, of which 3 were waited for; matrix products, arithmetic and copies ran while one was open for 33% of the time, Pallas kernels for 0%

profile of v1, /device:TPU:1, one launch (start us, length us, event | category | flops | bytes accessed | tf_op | source)
XLA Modules:
  0.0 533.4 jit_solution(10372606073273615850)
XLA Ops:
  10.3 4.9 gather_fusion
  15.3 6.4 %gather_fusion.1 = bf16[128,4096]{1,0:T(8,128)(2,1)} fusion(bf16[512,4096]{1,0:T(8,128)(2,1)} %param.14, s32[1024]{0:T(1024)S(1)} %get-tuple-element.89), kind=kCustom, calls=%fused_computation.1.clone | custom fusion | bytes 2097664 | tf_op jit(solution)/shard_map/jit(_take)/gather | solution.py:140
  24.3 2.2 fusion.82
  27.6 4.2 collective-permute-start
  34.4 9.4 %slice.124 = bf16[1,3,4096]{2,1,0:T(4,128)(2,1)} reverse(bf16[1,3,4096]{2,1,0:T(4,128)(2,1)S(1)} %get-tuple-element.69), dimensions={1} | reverse | bytes 49152 | tf_op jit(solution)/shard_map/slice | solution.py:153
  52.3 2.1 multiply_convert_fusion
  57.0 3.0 copy.4142
  60.0 3.6 reshape.642
  85.0 10.1 %all-to-all-start.2 = ((bf16[32,1,128,128]{3,2,1,0:T(8,128)(2,1)}), bf16[32,1,128,128]{3,2,1,0:T(8,128)(2,1)S(1)}, u32[]{:S(2)}, u32[]{:S(2)}) async-start(bf16[32,1,128,128]{3,2,1,0:T(8,128)(2,1)} %constant_dynamic-update-slice_fusion.32), calls=%async_computation.2 | async-start | bytes 2097152 | tf_op jit(solution)/shard_map/all_to_all | solution.py:12
  174.4 9.8 %all-to-all-start = ((bf16[32,1,128,128]{3,2,1,0:T(8,128)(2,1)}), bf16[32,1,128,128]{3,2,1,0:T(8,128)(2,1)}, u32[]{:S(2)}, u32[]{:S(2)}) async-start(bf16[32,1,128,128]{3,2,1,0:T(8,128)(2,1)} %constant_dynamic-update-slice_fusion), calls=%async_computation | async-start | bytes 2097152 | tf_op jit(solution)/shard_map/all_to_all | solution.py:12
  189.4 6.9 %convolution_bitcast_fusion.1 = f32[1,2,64,128,128]{4,2,1,3,0:T(8,128)} fusion(f32[32,128,128,1]{2,1,0,3:T(8,128)S(1)} %bitcast.530, f32[1,64,32]{1,2,0:T(8,128)S(1)} %get-tuple-element.81, f32[1,64,32]{1,2,0:T(8,128)S(1)} %get-tuple-element.80), kind=kOutput, calls=%fused_computation.61 | convolution fusion | flops 402657280 | bytes 10502144 | tf_op jit(solution)/shard_map/rka,pabc->prkbc/dot_general | solution.py:77
  196.2 5.7 %convolution_bitcast_fusion = f32[1,2,64,128,128]{4,2,1,3,0:T(8,128)} fusion(bf16[32,1,128,128]{3,2,1,0:T(8,128)(2,1)S(1)} %all-to-all-done.2, f32[1,64,32]{1,2,0:T(8,128)S(1)} %get-tuple-element.81, f32[1,64,32]{1,2,0:T(8,128)S(1)} %get-tuple-element.80), kind=kOutput, calls=%fused_computation.60 | convolution fusion | flops 402657280 | bytes 9453568 | tf_op jit(solution)/shard_map/rka,pabc->prkbc/dot_general | solution.py:77
  201.9 3.8 convolution_bitcast_fusion.2
  205.7 10.9 %multiply_subtract_fusion.6 = (f32[1,1,64,128,128]{4,2,1,3,0:T(8,128)}, f32[1,1,64,128,128]{4,2,1,3,0:T(8,128)}, f32[1,1,64,128,128]{4,2,1,3,0:T(8,128)S(1)}, f3...) fusion(f32[1,2,64,128,128]{4,2,1,3,0:T(8,128)S(1)} %convolution_bitcast_fusion, ...), kind=kLoop, calls=%fused_computation.54 | loop fusion | flops 18874368 | bytes 50397184 | tf_op jit(solution)/shard_map/sub | solution.py:64
  216.7 8.4 %maximum_bitcast_fusion.5 = f32[2,64,128,128]{3,1,0,2:T(8,128)} fusion(f32[1,1,64,128,128]{4,2,1,3,0:T(8,128)} %get-tuple-element.63, f32[1,1,64,128,128]{4,2,1,3,0:T(8,128)} %get-tuple-element.64), kind=kLoop, calls=%fused_computation.9 | loop fusion | flops 2097152 | bytes 16777216 | tf_op jit(solution)/shard_map/reshape.39
  225.1 4.1 maximum_bitcast_fusion.1
  229.2 12.2 %fusion.33 = f32[1,2,64,128,128]{4,3,2,1,0:T(8,128)S(1)} fusion(f32[2,64,128,128]{3,1,0,2:T(8,128)} %maximum_bitcast_fusion.5, f32[1,2,128,128]{2,3,0,1:T(8,128)S(1)} %get-tuple-element.72, f32[1,2,128,128]{2,3,0,1:T(8,128)S(1)} %get-tuple-element.73), kind=kOutput, calls=%fused_computation.58 | convolution fusion | flops 3221291008 | bytes 17039360 | tf_op jit(solution)/shard_map/prkbc,rsbm->pskmc/dot_general | solution.py:79
  241.5 13.8 %fusion.27 = f32[1,2,64,128,128]{4,3,2,1,0:T(8,128)} fusion(f32[2,64,128,128]{3,1,0,2:T(8,128)S(1)} %copy-done.2, f32[1,2,128,128]{2,3,0,1:T(8,128)S(1)} %get-tuple-element.72, f32[1,2,128,128]{2,3,0,1:T(8,128)S(1)} %get-tuple-element.73), kind=kOutput, calls=%fused_computation.56 | convolution fusion | flops 3221291008 | bytes 17039360 | tf_op jit(solution)/shard_map/prkbc,rsbm->pskmc/dot_general | solution.py:79
  255.2 6.7 %maximum_bitcast_fusion = f32[2,64,128,128]{3,1,0,2:T(8,128)} fusion(f32[1,1,64,128,128]{4,2,1,3,0:T(8,128)} %get-tuple-element.14, f32[1,1,64,128,128]{4,2,1,3,0:T(8,128)S(1)} %copy-done.10), kind=kLoop, calls=%fused_computation.2 | loop fusion | flops 2097152 | bytes 16777216 | tf_op jit(solution)/shard_map/reshape.23
  262.0 14.1 %fusion.24 = f32[1,2,64,128,128]{4,3,2,1,0:T(8,128)} fusion(f32[2,64,128,128]{3,1,0,2:T(8,128)} %maximum_bitcast_fusion, f32[1,2,128,128]{2,3,0,1:T(8,128)S(1)} %get-tuple-element.72, f32[1,2,128,128]{2,3,0,1:T(8,128)S(1)} %get-tuple-element.73), kind=kOutput, calls=%fused_computation.55 | convolution fusion | flops 3221291008 | bytes 17039360 | tf_op jit(solution)/shard_map/prkbc,rsbm->pskmc/dot_general | solution.py:79
  276.0 11.9 %multiply_subtract_fusion.4 = (f32[1,1,64,128,128]{4,3,2,1,0:T(8,128)}, f32[1,1,64,128,128]{4,3,2,1,0:T(8,128)}, f32[1,1,64,128,128]{4,3,2,1,0:T(8,128)}, f32[1,1,64,128,128]{4,3,2,1,0:T(8,128)}) fusion(f32[1,2,64,128,128]{4,3,2,1,0:T(8,128)} %fusion.24, f32[1,2,64,128,128]{4,3,2,1,0:T(8,128)} %fusion.27, f32[1,2,64,128,128]{4,3,2,1,0:T(8,128)S(1)} %fusion.33), kind=kLoop, calls=%fused_computation.50 | loop fusion | flops 12582912 | bytes 41943040 | tf_op jit(solution)/shard_map/sub | solution.py:107
  287.9 6.9 %fusion.36 = f32[2,128,64,128]{3,1,2,0:T(8,128)S(1)} fusion(f32[1,2,128,128]{2,3,0,1:T(8,128)S(1)} %copy-done.32, f32[1,2,128,128]{2,3,0,1:T(8,128)S(1)} %copy-done.31, f32[1,1,64,128,128]{4,3,2,1,0:T(8,128)} %get-tuple-element.21, f32[1,1,64,128,128]{4,3,2,1,0:T(8,128)} %get-tuple-element.22), kind=kOutput, calls=%fused_computation.59 | convolution fusion | flops 3223388160 | bytes 17039360 | tf_op jit(solution)/shard_map/pskmc,stmb->ptkbc/dot_general | solution.py:88
  294.8 4.9 copy.4265
  299.7 8.9 %fusion.30 = f32[2,128,64,128]{3,1,2,0:T(8,128)} fusion(f32[1,2,128,128]{2,3,0,1:T(8,128)S(1)} %copy-done.32, f32[1,2,128,128]{2,3,0,1:T(8,128)S(1)} %copy-done.31, f32[1,1,64,128,128]{4,3,2,1,0:T(8,128)} %get-tuple-element.8, f32[1,1,64,128,128]{4,3,2,1,0:T(8,128)} %get-tuple-element.7), kind=kOutput, calls=%fused_computation.57 | convolution fusion | flops 3223388160 | bytes 17039360 | tf_op jit(solution)/shard_map/pskmc,stmb->ptkbc/dot_general | solution.py:88
  308.6 8.3 %copy.4266 = f32[2,128,64,128]{3,2,0,1:T(8,128)S(1)} copy(f32[2,128,64,128]{3,1,2,0:T(8,128)} %fusion.30) | data formatting | bytes 16777216 | tf_op jit(solution)/shard_map/pskmc,stmb->ptkbc/dot_general | solution.py:88
  316.9 6.8 %multiply_subtract_fusion.3 = (f32[1,1,64,128,128]{4,2,1,3,0:T(8,128)S(1)}, f32[1,1,64,128,128]{4,2,1,3,0:T(8,128)}, f32[1,1,64,128,128]{4,2,1,3,0:T(8,128)}, f32[1,1,64,128,128]{4,2,1,3,0:T(8,128)}) fusion(f32[1,2,64,128,128]{4,2,1,3,0:T(8,128)S(1)} %bitcast.532, f32[64,128]{0,1:T(8,128)S(1)} %copy-done.26, f32[64,128]{0,1:T(8,128)S(1)} %get-tuple-element.92, ...), kind=kLoop, calls=%fused_computation.48 | loop fusion | flops 12582912 | bytes 33619968 | tf_op jit(solution)/shard_map/sub | solution.py:64
  323.7 4.8 fusion.62
  330.7 2.4 fusion.63
  334.4 2.8 fusion.59
  337.2 16.7 %copy.4268 = bf16[1,4096,128]{2,0,1:T(2,128)(2,1)S(1)} copy(bf16[1,4096,128]{2,1,0:T(8,128)(2,1)S(1)} %get-tuple-element.84) | data formatting | bytes 2097152 | tf_op jit(solution)/shard_map/convert_element_type | solution.py:109
  354.4 22.4 %reduce.4 = bf16[4096,128]{1,0:T(8,128)(2,1)S(1)} reduce(bf16[4096,1,128]{2,1,0:T(2,128)(2,1)S(1)} %bitcast.536, bf16[]{:T(256)} %broadcast.617), dimensions={1}, to_apply=%bitcast.529.reduce_sub_computation | reduce | bytes 2097154
  377.9 9.7 %all-to-all-start.1 = ((bf16[32,2,8192]{2,1,0:T(2,128)(2,1)}), bf16[32,2,8192]{2,1,0:T(2,128)(2,1)}, u32[]{:S(2)}, u32[]{:S(2)}) async-start(bf16[32,2,8192]{2,1,0:T(2,128)(2,1)} %reshape.744), calls=%async_computation.1 | async-start | bytes 2097152 | tf_op jit(solution)/shard_map/all_to_all | solution.py:129
  387.6 4.8 copy.4151
  392.4 3.0 copy.4152
  395.4 3.6 reshape.646
  399.1 3.6 reshape.644
  402.7 16.7 %copy.4267 = bf16[1,4096,128]{2,0,1:T(2,128)(2,1)S(1)} copy(bf16[1,4096,128]{2,1,0:T(8,128)(2,1)S(1)} %copy-done.20) | data formatting | bytes 2097152 | tf_op jit(solution)/shard_map/convert_element_type | solution.py:109
  419.4 22.4 %reduce.3 = bf16[4096,128]{1,0:T(8,128)(2,1)S(1)} reduce(bf16[4096,1,128]{2,1,0:T(2,128)(2,1)S(1)} %bitcast.537, bf16[]{:T(256)} %broadcast.617), dimensions={1}, to_apply=%bitcast.528.reduce_sub_computation | reduce | bytes 2097154
  442.9 9.4 %all-to-all-start.3 = ((bf16[32,2,8192]{2,1,0:T(2,128)(2,1)}), bf16[32,2,8192]{2,1,0:T(2,128)(2,1)S(1)}, u32[]{:S(2)}, u32[]{:S(2)}) async-start(bf16[32,2,8192]{2,1,0:T(2,128)(2,1)} %reshape.742), calls=%async_computation.3 | async-start | bytes 2097152 | tf_op jit(solution)/shard_map/all_to_all | solution.py:129
  452.3 4.3 reshape.745
  461.1 5.5 %all-to-all-done.3 = bf16[32,2,8192]{2,1,0:T(2,128)(2,1)S(1)} async-done(((bf16[32,2,8192]{2,1,0:T(2,128)(2,1)}), bf16[32,2,8192]{2,1,0:T(2,128)(2,1)S(1)}, u32[]{:S(2)}, u32[]{:S(2)}) %all-to-all-start.3) | async-done | bytes 1048608 | tf_op jit(solution)/shard_map/all_to_all | solution.py:129
  472.9 3.3 collective-permute-done.1
  485.6 3.0 copy.4159
  488.6 3.7 reshape.640
  492.4 2.5 fusion.61
  494.9 2.3 fusion.83
  497.2 26.7 %reduce-scatter.2.cloned.1.call-done = bf16[128,1024]{1,0:T(8,128)(2,1)} async-done(((bf16[128,4096]{1,0:T(8,128)(2,1)}), bf16[128,1024]{1,0:T(8,128)(2,1)}) %reduce-scatter.2.cloned.1.call-update) | async-done | bytes 262160 | tf_op jit(solution)/shard_map/reduce_scatter | solution.py:177
  523.9 2.2 dynamic-slice_multiply_fusion
  (302 shorter events, 152.5 us)
Async XLA Ops:
  7.2 182.2 %copy-start = (f32[4096,128]{1,0:T(8,128)S(1)}, f32[4096,128]{1,0:T(8,128)}, u32[]{:S(2)}) copy-start(f32[4096,128]{1,0:T(8,128)} %param.17) | copy-start | bytes 6291460
  10.3 14.0 %copy-start.40 = (pred[128]{0:T(512)(128)(4,1)}, pred[128]{0:T(512)(128)(4,1)S(1)}, u32[]{:S(2)}) copy-start(pred[128]{0:T(512)(128)(4,1)S(1)} %get-tuple-element.5) | copy-start | bytes 388
  10.3 14.0 %copy-start.42 = (pred[128]{0:T(512)(128)(4,1)}, pred[128]{0:T(512)(128)(4,1)S(1)}, u32[]{:S(2)}) copy-start(pred[128]{0:T(512)(128)(4,1)S(1)} %get-tuple-element.86) | copy-start | bytes 388
  15.3 9.0 %copy-start.4 = (bf16[128,4096]{1,0:T(8,128)(2,1)}, bf16[128,4096]{1,0:T(8,128)(2,1)S(1)}, u32[]{:S(2)}) copy-start(bf16[128,4096]{1,0:T(8,128)(2,1)S(1)} %gather_fusion) | copy-start | bytes 3145732
  15.3 9.0 %copy-start.38 = (f32[4096]{0:T(1024)S(1)}, f32[4096]{0:T(1024)}, u32[]{:S(2)}) copy-start(f32[4096]{0:T(1024)} %param.15) | copy-start | bytes 49156
  21.7 2.7 copy-start.6
  24.3 2.2 copy-start.46
  24.3 8.4 %copy-start.33 = (bf16[3,3,4096]{2,1,0:T(4,128)(2,1)S(1)}, bf16[3,3,4096]{2,1,0:T(4,128)(2,1)}, u32[]{:S(2)}) copy-start(bf16[3,3,4096]{2,1,0:T(4,128)(2,1)} %param.16) | copy-start | bytes 221188
  27.6 17.9 %collective-permute-start = (bf16[1,2,4096]{2,1,0:T(2,128)(2,1)S(1)}, bf16[1,2,4096]{2,1,0:T(2,128)(2,1)S(1)}, u32[]{:S(2)}, u32[]{:S(2)}) collective-permute-start(bf16[1,2,4096]{2,1,0:T(2,128)(2,1)S(1)} %slice.214), channel_id=1, source_target_pairs={{0,1},{1,2},{2,3},{3,4},{4,5},{5,6},{6,7},{7,8},{8,9},{9,10},{10,1... | collective-permute-start | bytes 49160 | tf_op jit(solution)/shard_map/ppermute | solution.py:23
  31.8 1.6 copy-start.27
  48.6 2.8 copy-start.44
  52.3 2.1 copy-start.12
  54.5 1.6 copy-start.37
  60.0 3.6 copy-start.21
  85.0 89.3 %all-to-all-start.2 = ((bf16[32,1,128,128]{3,2,1,0:T(8,128)(2,1)}), bf16[32,1,128,128]{3,2,1,0:T(8,128)(2,1)S(1)}, u32[]{:S(2)}, u32[]{:S(2)}) async-start(bf16[32,1,128,128]{3,2,1,0:T(8,128)(2,1)} %constant_dynamic-update-slice_fusion.32), calls=%async_computation.2 | async-start | bytes 2097152 | tf_op jit(solution)/shard_map/all_to_all | solution.py:12
  134.5 32.8 %copy-start.29 = (bf16[1,136,128]{2,1,0:T(8,128)(2,1)S(1)}, bf16[1,136,128]{2,1,0:T(8,128)(2,1)}, u32[]{:S(2)}) copy-start(bf16[1,136,128]{2,1,0:T(8,128)(2,1)} %reshape.604) | copy-start | bytes 104452
  135.1 34.1 %copy-start.30 = (bf16[1,136,128]{2,1,0:T(8,128)(2,1)S(1)}, bf16[1,136,128]{2,1,0:T(8,128)(2,1)}, u32[]{:S(2)}) copy-start(bf16[1,136,128]{2,1,0:T(8,128)(2,1)} %reshape.608) | copy-start | bytes 104452
  174.4 27.6 %all-to-all-start = ((bf16[32,1,128,128]{3,2,1,0:T(8,128)(2,1)}), bf16[32,1,128,128]{3,2,1,0:T(8,128)(2,1)}, u32[]{:S(2)}, u32[]{:S(2)}) async-start(bf16[32,1,128,128]{3,2,1,0:T(8,128)(2,1)} %constant_dynamic-update-slice_fusion), calls=%async_computation | async-start | bytes 2097152 | tf_op jit(solution)/shard_map/all_to_all | solution.py:12
  201.9 3.8 copy-start.25
  201.9 3.8 copy-start.3
  229.2 12.2 %copy-start.2 = (f32[2,64,128,128]{3,1,0,2:T(8,128)S(1)}, f32[2,64,128,128]{3,1,0,2:T(8,128)}, u32[]{:S(2)}) copy-start(f32[2,64,128,128]{3,1,0,2:T(8,128)} %maximum_bitcast_fusion.1) | copy-start | bytes 25165828
  241.4 13.8 %copy-start.10 = (f32[1,1,64,128,128]{4,2,1,3,0:T(8,128)S(1)}, f32[1,1,64,128,128]{4,2,1,3,0:T(8,128)}, u32[]{:S(2)}) copy-start(f32[1,1,64,128,128]{4,2,1,3,0:T(8,128)} %get-tuple-element.13) | copy-start | bytes 12582916
  276.0 11.9 %copy-start.31 = (f32[1,2,128,128]{2,3,0,1:T(8,128)S(1)}, f32[1,2,128,128]{2,3,0,1:T(8,128)}, u32[]{:S(2)}) copy-start(f32[1,2,128,128]{2,3,0,1:T(8,128)} %get-tuple-element.71) | copy-start | bytes 393220
  276.0 11.9 %copy-start.32 = (f32[1,2,128,128]{2,3,0,1:T(8,128)S(1)}, f32[1,2,128,128]{2,3,0,1:T(8,128)}, u32[]{:S(2)}) copy-start(f32[1,2,128,128]{2,3,0,1:T(8,128)} %get-tuple-element.74) | copy-start | bytes 393220
  308.6 8.3 %copy-start.26 = (f32[64,128]{0,1:T(8,128)S(1)}, f32[64,128]{0,1:T(8,128)}, u32[]{:S(2)}) copy-start(f32[64,128]{0,1:T(8,128)} %fusion.117) | copy-start | bytes 98308
  316.9 6.8 %copy-start.28 = (f32[1,32,64]{2,1,0:T(8,128)S(1)}, f32[1,32,64]{2,1,0:T(8,128)}, u32[]{:S(2)}) copy-start(f32[1,32,64]{2,1,0:T(8,128)} %copy.4136) | copy-start | bytes 24580
  328.5 2.2 copy-start.11
  377.9 65.0 %all-to-all-start.1 = ((bf16[32,2,8192]{2,1,0:T(2,128)(2,1)}), bf16[32,2,8192]{2,1,0:T(2,128)(2,1)}, u32[]{:S(2)}, u32[]{:S(2)}) async-start(bf16[32,2,8192]{2,1,0:T(2,128)(2,1)} %reshape.744), calls=%async_computation.1 | async-start | bytes 2097152 | tf_op jit(solution)/shard_map/all_to_all | solution.py:129
  387.6 4.8 copy-start.13
  399.1 3.6 copy-start.20
  442.9 23.7 %all-to-all-start.3 = ((bf16[32,2,8192]{2,1,0:T(2,128)(2,1)}), bf16[32,2,8192]{2,1,0:T(2,128)(2,1)S(1)}, u32[]{:S(2)}, u32[]{:S(2)}) async-start(bf16[32,2,8192]{2,1,0:T(2,128)(2,1)} %reshape.742), calls=%async_computation.3 | async-start | bytes 2097152 | tf_op jit(solution)/shard_map/all_to_all | solution.py:129
  452.3 71.7 %reduce-scatter.2.cloned.1.call-start = ((), (), s32[]{:S(2)}) async-start(), calls=%async_computation.5 | async-start | bytes 1310720 | tf_op jit(solution)/shard_map/reduce_scatter | solution.py:177
  467.6 1.6 copy-start.14
  471.3 5.0 copy-start.15
  471.4 4.8 collective-permute-start.1
  476.8 1.6 copy-start.19
  478.9 1.5 copy-start.16
  481.7 1.4 copy-start.35
  483.1 1.4 copy-start.39
  488.6 3.7 copy-start.5
  488.6 3.7 copy-start.7
  488.6 3.7 copy-start.41
  488.6 3.7 copy-start.43
  492.4 2.5 copy-start.8
  492.4 2.6 copy-start.9
  492.4 2.6 copy-start.47
  492.4 2.6 copy-start.49
  494.9 31.2 %copy-start.1 = (f32[4096,128]{1,0:T(8,128)S(1)}, f32[4096,128]{1,0:T(8,128)}, u32[]{:S(2)}) copy-start(f32[4096,128]{1,0:T(8,128)} %param.17) | copy-start | bytes 6291460
  (9 other events, 10.2 us)
Sparse Core Ops, SparseCore 0:
  497.3 26.5 reduce-scatter.1
